TPU v7x, 512 devices: a whole 4x4x16 slice. The times are simulated.
512 devices in a mesh: gx: 128 (over y_hi, z, x), trait: 4 (over y_lo, core).
Axes of the slice: x: 4, y: 4 (y_hi: 2, y_lo: 2; y = y_hi * 2 + y_lo), z: 16, core: 2. Of those that a mesh axis runs over, the one named last changes fastest.
Arguments:
- initial: float32 [1024, 128, 1024], P('gx', None, 'trait'), may hold values from 0.2 to 2
- section_one: float32 [1024, 128, 1024], P('gx', None, 'trait'), may hold values from 0.2 to 2
- section_two: float32 [1024, 128, 1024], P('gx', None, 'trait'), may hold values from 0.2 to 2
- kernels: bfloat16 [2, 1024, 1024], P(None, None, 'trait'), may hold values from -0.1875 to 0.1875
- growth: float32 [1024], P('trait'), may hold values from -3 to 3
- death_rate: float32 [1024], P('trait'), may hold values from 0.5 to 8
Outputs:
- new_one: float32 [1024, 128, 1024], P('gx', None, 'trait')
- new_two: float32 [1024, 128, 1024], P('gx', None, 'trait')
All inputs are finite; a program needn't handle non-finite values.
Results may differ from a plain program's by a relative error of at most 0.002.
Values may be sent and summed in bfloat16 or wider, within the bound.
A program may use at most 64 MiB of HBM per device.

v0:
```python
import jax
import jax.numpy as jnp
from jax import lax
from jax.sharding import PartitionSpec as P

DIFFUSION = 0.25
STEP_SIZE = 0.5


def with_halo(cells, sides, width):
    for axis, dim in sides:
        count = lax.axis_size(axis)
        head = lax.slice_in_dim(cells, 0, width, axis=dim)
        tail = lax.slice_in_dim(cells, cells.shape[dim] - width, cells.shape[dim], axis=dim)
        cells = jnp.concatenate(
            [
                lax.ppermute(tail, axis, [(i, (i + 1) % count) for i in range(count)]),
                cells,
                lax.ppermute(head, axis, [((i + 1) % count, i) for i in range(count)]),
            ],
            axis=dim,
        )
    return cells


def local(initial, section_one, section_two, kernels, growth, death_rate):
    first_dt = STEP_SIZE / 3.0
    second_dt = 2.0 * STEP_SIZE / 3.0

    def products(core):
        xcount, ycount, owned = core.shape
        flat = core.astype(jnp.bfloat16).reshape(xcount * ycount, owned)
        piece = lax.all_gather(flat, "trait", axis=1, tiled=True)
        compete = jnp.dot(piece, kernels[0], preferred_element_type=jnp.float32)
        mutate = jnp.dot(piece, kernels[1], preferred_element_type=jnp.float32)
        compete = compete.astype(jnp.bfloat16)
        mutate = mutate.astype(jnp.bfloat16)
        return (
            compete.astype(jnp.float32).reshape(xcount, ycount, owned),
            mutate.astype(jnp.float32).reshape(xcount, ycount, owned),
        )

    def explicit(padded):
        core = padded[1:-1]
        lapl = padded[2:] + padded[:-2] + jnp.roll(core, 1, 1) + jnp.roll(core, -1, 1) - 4.0 * core
        compete, mutate = products(core)
        return DIFFUSION * lapl + core * (growth - compete) + mutate - core

    padded_pair = with_halo(jnp.stack([section_one, section_two]), (("gx", 1),), 1)
    expl_one = explicit(padded_pair[0])
    expl_two = explicit(padded_pair[1])
    full_one = expl_one - death_rate * section_one
    full_two = expl_two - death_rate * section_two
    result = (
        initial
        + first_dt * death_rate * section_one
        + STEP_SIZE * (5.0 / 12.0 * full_one - 1.0 / 12.0 * full_two)
    ) / (1.0 + first_dt * death_rate)
    new_one, full_one, full_two = (result, full_one, full_two)
    padded_new = with_halo(new_one, (("gx", 0),), 1)
    expl_new = explicit(padded_new)
    new_two = (
        new_one
        + second_dt * (expl_new - expl_one)
        + second_dt * death_rate * section_two
        + STEP_SIZE / 3.0 * (full_one + full_two)
    ) / (1.0 + second_dt * death_rate)
    return (new_one, new_two)


def solution(mesh):
    in_specs = (
        P("gx", None, "trait"),
        P("gx", None, "trait"),
        P("gx", None, "trait"),
        P(None, None, "trait"),
        P("trait"),
        P("trait"),
    )
    out_specs = (P("gx", None, "trait"), P("gx", None, "trait"))
    return jax.shard_map(local, mesh=mesh, in_specs=in_specs, out_specs=out_specs, check_vma=False)
```

profile of v0, /device:TPU:1, one launch (start us, length us, event | category | flops | bytes accessed | tf_op | source)
XLA Modules:
  0.0 153.2 jit_solution(10018028069680694838)
XLA Ops:
  7.2 0.0 copy-start
  7.2 0.0 copy-start.1
  7.2 0.0 all-gather.4.cloned.1.call-start
  7.2 2.2 %convert_element_type.41 = bf16[8,128,256]{2,1,0:T(8,128)(2,1)} convert(f32[8,128,256]{2,1,0:T(8,128)} %param.7) | non-fusion elementwise | flops 262144 | bytes 1572864 | tf_op jit(solution)/shard_map/convert_element_type | solution.py:32
  9.4 0.0 all-gather.4.cloned.1.call-update
  9.5 0.0 copy-start.15
  9.5 0.0 all-gather.6.cloned.1.call-start
  9.5 0.0 copy-done.1
  9.5 0.8 convert_element_type.45
  10.4 0.0 all-gather.6.cloned.1.call-update
  10.4 0.0 all-gather.8.cloned.1.call-start
  10.5 0.0 copy-done
  10.5 16.8 %collective-permute-start = (f32[2,1,128,256]{3,2,1,0:T(8,128)S(1)}, f32[2,1,128,256]{3,2,1,0:T(8,128)S(1)}, u32[]{:S(2)}, u32[]{:S(2)}) collective-permute-start(f32[2,1,128,256]{3,2,1,0:T(8,128)S(1)} %get-tuple-element.6), channel_id=1, source_target_pairs={{4,0},{8,4},{12,8},{16,12},{20,16},{24,20},{28,24},{32,28},{36,32}... | collective-permute-start | bytes 786440 | tf_op jit(solution)/shard_map/ppermute | solution.py:19
  27.3 1.9 %collective-permute-start.1 = (f32[2,1,128,256]{3,2,1,0:T(8,128)S(1)}, f32[2,1,128,256]{3,2,1,0:T(8,128)S(1)}, u32[]{:S(2)}, u32[]{:S(2)}) collective-permute-start(f32[2,1,128,256]{3,2,1,0:T(8,128)S(1)} %get-tuple-element.7), channel_id=1, source_target_pairs={{0,4},{4,8},{8,12},{12,16},{16,20},{20,24},{24,28},{28,32},{32,36}... | collective-permute-start | bytes 786440 | tf_op jit(solution)/shard_map/ppermute | solution.py:17
  29.2 0.0 copy-done.15
  29.2 0.6 broadcast_multiply_fusion
  29.9 2.2 %fusion.54 = (f32[8,127,256]{2,1,0:T(8,128)}, f32[8,127,256]{2,1,0:T(8,128)}, f32[8,127,256]{2,1,0:T(8,128)}, f32[8,127,256]{2,1,0:T(8,128)}) fusion(f32[8,128,256]{2,1,0:T(8,128)S(1)} %copy-done.1, f32[8,128,256]{2,1,0:T(8,128)S(1)} %copy-done), kind=kLoop, calls=%fused_computation.76 | loop fusion | bytes 8323072 | tf_op jit(solution)/shard_map/jit(_roll_static)/slice | solution.py:45
  32.0 26.1 %all-gather.4.cloned.1.call-done = bf16[1024,1024]{1,0:T(8,128)(2,1)} async-done(((bf16[1024,256]{1,0:T(8,128)(2,1)}), bf16[1024,1024]{1,0:T(8,128)(2,1)}) %all-gather.4.cloned.1.call-update) | async-done | bytes 2097168 | tf_op jit(solution)/shard_map/all_gather | solution.py:33
  58.2 3.3 %convolution_convert_fusion.4 = bf16[1024,256]{1,0:T(8,128)(2,1)} fusion(bf16[1024,1024]{1,0:T(8,128)(2,1)} %all-gather.4.cloned.1.call-done, bf16[2,1024,256]{2,1,0:T(8,128)(2,1)} %param.9), kind=kOutput, calls=%fused_computation.4 | convolution fusion | flops 537133056 | bytes 3145728 | tf_op jit(solution)/shard_map/dot_general | solution.py:35
  61.5 0.0 copy-done.21
  61.5 0.0 copy-done.24
  61.5 1.5 convolution_convert_fusion.5
  63.0 29.3 %all-gather.6.cloned.1.call-done = bf16[1024,1024]{1,0:T(8,128)(2,1)} async-done(((bf16[1024,256]{1,0:T(8,128)(2,1)}), bf16[1024,1024]{1,0:T(8,128)(2,1)}) %all-gather.6.cloned.1.call-update) | async-done | bytes 2097168 | tf_op jit(solution)/shard_map/all_gather | solution.py:33
  92.3 2.5 %convolution_convert_fusion.2 = bf16[1024,256]{1,0:T(8,128)(2,1)S(1)} fusion(bf16[1024,1024]{1,0:T(8,128)(2,1)} %all-gather.6.cloned.1.call-done, bf16[2,1024,256]{2,1,0:T(8,128)(2,1)} %param.9), kind=kOutput, calls=%fused_computation.2 | convolution fusion | flops 537133056 | bytes 3145728 | tf_op jit(solution)/shard_map/dot_general | solution.py:35
  94.9 0.0 copy-done.22
  94.9 0.1 copy-done.25
  95.0 0.0 copy-start.11
  95.0 0.0 copy-start.12
  95.0 0.0 copy-start.13
  95.0 0.0 copy-start.17
  95.0 0.7 convolution_convert_fusion.3
  95.7 0.0 collective-permute-done
  95.7 0.0 collective-permute-done.1
  95.7 0.0 copy-start.14
  95.8 0.7 copy-done.14
  96.5 0.0 copy-done.7
  96.5 0.0 copy-done.8
  96.5 0.4 copy-done.9
  96.9 0.3 copy-done.10
  97.2 0.3 copy-done.11
  97.5 0.1 copy-done.12
  97.7 0.2 copy-done.13
  97.8 0.0 copy-done.17
  97.8 3.5 %fusion.47 = (bf16[8,128,256]{2,1,0:T(8,128)(2,1)}, f32[8,128,256]{2,1,0:T(8,128)S(1)}, f32[8,128,256]{2,1,0:T(8,128)}, f32[8,128,256]{2,1,0:T(8,128)}) fusion(f32[256]{0:T(256)S(1)} %get-tuple-element.23, f32[8,128,256]{2,1,0:T(8,128)S(1)} %copy-done, f32[256]{0:T(256)S(1)} %copy-done.15, f32[8,128,256]{2,1,0:T(8,128)S(1)} %copy-done.11, ...), kind=kLoop, calls=%fused_computation.71 | loop fusion | flops 13369344 | bytes 15732736 | tf_op jit(solution)/shard_map/convert_element_type | solution.py:32
  101.4 0.0 all-gather.8.cloned.1.call-update
  101.4 0.7 fusion.52
  102.1 9.9 %collective-permute-start.2 = (f32[1,128,256]{2,1,0:T(8,128)}, f32[1,128,256]{2,1,0:T(8,128)S(1)}, u32[]{:S(2)}, u32[]{:S(2)}) collective-permute-start(f32[1,128,256]{2,1,0:T(8,128)} %get-tuple-element.12), channel_id=1, source_target_pairs={{4,0},{8,4},{12,8},{16,12},{20,16},{24,20},{28,24},{32,28},{36,32}... | collective-permute-start | bytes 393224 | tf_op jit(solution)/shard_map/ppermute | solution.py:19
  112.1 1.9 %collective-permute-start.3 = (f32[1,128,256]{2,1,0:T(8,128)S(1)}, f32[1,128,256]{2,1,0:T(8,128)S(1)}, u32[]{:S(2)}, u32[]{:S(2)}) collective-permute-start(f32[1,128,256]{2,1,0:T(8,128)S(1)} %get-tuple-element.13), channel_id=1, source_target_pairs={{0,4},{4,8},{8,12},{12,16},{16,20},{20,24},{24,28},{28,32},{32,36}... | collective-permute-start | bytes 393224 | tf_op jit(solution)/shard_map/ppermute | solution.py:17
  114.0 1.5 fusion.50
  115.5 24.3 %all-gather.8.cloned.1.call-done = bf16[1024,1024]{1,0:T(8,128)(2,1)} async-done(((bf16[1024,256]{1,0:T(8,128)(2,1)}), bf16[1024,1024]{1,0:T(8,128)(2,1)}) %all-gather.8.cloned.1.call-update) | async-done | bytes 2097168 | tf_op jit(solution)/shard_map/all_gather | solution.py:33
  139.8 2.5 %convolution_convert_fusion = bf16[1024,256]{1,0:T(8,128)(2,1)S(1)} fusion(bf16[1024,1024]{1,0:T(8,128)(2,1)} %all-gather.8.cloned.1.call-done, bf16[2,1024,256]{2,1,0:T(8,128)(2,1)} %param.9), kind=kOutput, calls=%fused_computation | convolution fusion | flops 537133056 | bytes 3145728 | tf_op jit(solution)/shard_map/dot_general | solution.py:35
  142.4 0.1 copy-done.26
  142.5 0.0 copy-start.16
  142.5 0.0 copy-start.18
  142.5 0.7 convolution_convert_fusion.1
  143.2 0.0 collective-permute-done.2
  143.2 0.0 collective-permute-done.3
  143.3 0.0 copy-done.2
  143.3 0.4 copy-done.3
  143.7 0.3 copy-done.4
  144.0 0.3 copy-done.5
  144.3 0.3 copy-done.6
  144.6 0.0 copy-done.20
  144.7 2.0 %fusion.13 = f32[8,128,256]{2,1,0:T(8,128)} fusion(f32[8,128,256]{2,1,0:T(8,128)S(1)} %get-tuple-element.3, f32[8,128,256]{2,1,0:T(8,128)S(1)} %copy-done.3, f32[1,128,256]{2,1,0:T(8,128)S(1)} %collective-permute-done.3, f32[1,128,256]{2,1,0:T(8,128)S(1)} %collective-permute-done.2, f32[8,127,256]{2,1,0:T(8,128)S(1)} %copy-done.6, ...), kind=kLoop, calls=%fused_computation.20 | loop fusion | flops 7340032 | bytes 9703424 | tf_op jit(solution)/shard_map/div | solution.py:62
  (24 shorter events, 0.1 us)
Async XLA Ops:
  7.2 3.3 %copy-start = (f32[8,128,256]{2,1,0:T(8,128)S(1)}, f32[8,128,256]{2,1,0:T(8,128)}, u32[]{:S(2)}) copy-start(f32[8,128,256]{2,1,0:T(8,128)} %param.7) | copy-start | bytes 3145732
  7.2 2.4 %copy-start.1 = (f32[8,128,256]{2,1,0:T(8,128)S(1)}, f32[8,128,256]{2,1,0:T(8,128)}, u32[]{:S(2)}) copy-start(f32[8,128,256]{2,1,0:T(8,128)} %param.8) | copy-start | bytes 3145732
  7.2 51.0 %all-gather.4.cloned.1.call-start = ((), (), s32[]{:S(2)}) async-start(), calls=%async_computation | async-start | bytes 2621440 | tf_op jit(solution)/shard_map/all_gather | solution.py:33
  9.5 19.8 %copy-start.15 = (f32[256]{0:T(256)S(1)}, f32[256]{0:T(256)}, u32[]{:S(2)}) copy-start(f32[256]{0:T(256)} %param.11) | copy-start | bytes 3076
  9.5 82.8 %all-gather.6.cloned.1.call-start = ((), (), s32[]{:S(2)}) async-start(), calls=%async_computation.1 | async-start | bytes 2621440 | tf_op jit(solution)/shard_map/all_gather | solution.py:33
  10.4 129.4 %all-gather.8.cloned.1.call-start = ((), (), s32[]{:S(2)}) async-start(), calls=%async_computation.2 | async-start | bytes 2621440 | tf_op jit(solution)/shard_map/all_gather | solution.py:33
  10.5 85.2 %collective-permute-start = (f32[2,1,128,256]{3,2,1,0:T(8,128)S(1)}, f32[2,1,128,256]{3,2,1,0:T(8,128)S(1)}, u32[]{:S(2)}, u32[]{:S(2)}) collective-permute-start(f32[2,1,128,256]{3,2,1,0:T(8,128)S(1)} %get-tuple-element.6), channel_id=1, source_target_pairs={{4,0},{8,4},{12,8},{16,12},{20,16},{24,20},{28,24},{32,28},{36,32}... | collective-permute-start | bytes 786440 | tf_op jit(solution)/shard_map/ppermute | solution.py:19
  27.3 68.4 %collective-permute-start.1 = (f32[2,1,128,256]{3,2,1,0:T(8,128)S(1)}, f32[2,1,128,256]{3,2,1,0:T(8,128)S(1)}, u32[]{:S(2)}, u32[]{:S(2)}) collective-permute-start(f32[2,1,128,256]{3,2,1,0:T(8,128)S(1)} %get-tuple-element.7), channel_id=1, source_target_pairs={{0,4},{4,8},{8,12},{12,16},{16,20},{20,24},{24,28},{28,32},{32,36}... | collective-permute-start | bytes 786440 | tf_op jit(solution)/shard_map/ppermute | solution.py:17
  58.2 3.3 %copy-start.21 = (bf16[1024,1024]{1,0:T(8,128)(2,1)S(1)}, bf16[1024,1024]{1,0:T(8,128)(2,1)}, u32[]{:S(2)}) copy-start(bf16[1024,1024]{1,0:T(8,128)(2,1)} %all-gather.4.cloned.1.call-done) | copy-start | bytes 6291460
  58.2 3.3 %copy-start.24 = (bf16[2,1024,256]{2,1,0:T(8,128)(2,1)S(1)}, bf16[2,1024,256]{2,1,0:T(8,128)(2,1)}, u32[]{:S(2)}) copy-start(bf16[2,1024,256]{2,1,0:T(8,128)(2,1)} %param.9) | copy-start | bytes 3145732
  92.3 2.5 %copy-start.22 = (bf16[1024,1024]{1,0:T(8,128)(2,1)S(1)}, bf16[1024,1024]{1,0:T(8,128)(2,1)}, u32[]{:S(2)}) copy-start(bf16[1024,1024]{1,0:T(8,128)(2,1)} %all-gather.6.cloned.1.call-done) | copy-start | bytes 6291460
  92.3 2.6 %copy-start.25 = (bf16[2,1024,256]{2,1,0:T(8,128)(2,1)S(1)}, bf16[2,1024,256]{2,1,0:T(8,128)(2,1)}, u32[]{:S(2)}) copy-start(bf16[2,1024,256]{2,1,0:T(8,128)(2,1)} %param.9) | copy-start | bytes 3145732
  95.0 1.5 copy-start.7
  95.0 1.5 %copy-start.8 = (f32[8,127,256]{2,1,0:T(8,128)S(1)}, f32[8,127,256]{2,1,0:T(8,128)}, u32[]{:S(2)}) copy-start(f32[8,127,256]{2,1,0:T(8,128)} %get-tuple-element.17) | copy-start | bytes 3121156
  95.0 1.9 %copy-start.9 = (f32[8,127,256]{2,1,0:T(8,128)S(1)}, f32[8,127,256]{2,1,0:T(8,128)}, u32[]{:S(2)}) copy-start(f32[8,127,256]{2,1,0:T(8,128)} %get-tuple-element.28) | copy-start | bytes 3121156
  95.0 2.3 %copy-start.10 = (f32[8,127,256]{2,1,0:T(8,128)S(1)}, f32[8,127,256]{2,1,0:T(8,128)}, u32[]{:S(2)}) copy-start(f32[8,127,256]{2,1,0:T(8,128)} %get-tuple-element.29) | copy-start | bytes 3121156
  95.0 2.6 %copy-start.11 = (f32[8,128,256]{2,1,0:T(8,128)S(1)}, f32[8,128,256]{2,1,0:T(8,128)}, u32[]{:S(2)}) copy-start(f32[8,128,256]{2,1,0:T(8,128)} %param.6) | copy-start | bytes 3145732
  95.0 2.7 %copy-start.12 = (bf16[1024,256]{1,0:T(8,128)(2,1)S(1)}, bf16[1024,256]{1,0:T(8,128)(2,1)}, u32[]{:S(2)}) copy-start(bf16[1024,256]{1,0:T(8,128)(2,1)} %convolution_convert_fusion.4) | copy-start | bytes 1572868
  95.0 2.8 %copy-start.13 = (bf16[1024,256]{1,0:T(8,128)(2,1)S(1)}, bf16[1024,256]{1,0:T(8,128)(2,1)}, u32[]{:S(2)}) copy-start(bf16[1024,256]{1,0:T(8,128)(2,1)} %convolution_convert_fusion.5) | copy-start | bytes 1572868
  95.0 2.8 %copy-start.17 = (f32[256]{0:T(256)S(1)}, f32[256]{0:T(256)}, u32[]{:S(2)}) copy-start(f32[256]{0:T(256)} %param.10) | copy-start | bytes 3076
  95.7 0.7 copy-start.14
  101.4 41.9 %copy-start.2 = (f32[8,128,256]{2,1,0:T(8,128)}, f32[8,128,256]{2,1,0:T(8,128)S(1)}, u32[]{:S(2)}) copy-start(f32[8,128,256]{2,1,0:T(8,128)S(1)} %get-tuple-element.3) | copy-start | bytes 3145732
  102.1 41.1 %collective-permute-start.2 = (f32[1,128,256]{2,1,0:T(8,128)}, f32[1,128,256]{2,1,0:T(8,128)S(1)}, u32[]{:S(2)}, u32[]{:S(2)}) collective-permute-start(f32[1,128,256]{2,1,0:T(8,128)} %get-tuple-element.12), channel_id=1, source_target_pairs={{4,0},{8,4},{12,8},{16,12},{20,16},{24,20},{28,24},{32,28},{36,32}... | collective-permute-start | bytes 393224 | tf_op jit(solution)/shard_map/ppermute | solution.py:19
  112.1 31.2 %collective-permute-start.3 = (f32[1,128,256]{2,1,0:T(8,128)S(1)}, f32[1,128,256]{2,1,0:T(8,128)S(1)}, u32[]{:S(2)}, u32[]{:S(2)}) collective-permute-start(f32[1,128,256]{2,1,0:T(8,128)S(1)} %get-tuple-element.13), channel_id=1, source_target_pairs={{0,4},{4,8},{8,12},{12,16},{16,20},{20,24},{24,28},{28,32},{32,36}... | collective-permute-start | bytes 393224 | tf_op jit(solution)/shard_map/ppermute | solution.py:17
  139.8 2.5 %copy-start.23 = (bf16[1024,1024]{1,0:T(8,128)(2,1)S(1)}, bf16[1024,1024]{1,0:T(8,128)(2,1)}, u32[]{:S(2)}) copy-start(bf16[1024,1024]{1,0:T(8,128)(2,1)} %all-gather.8.cloned.1.call-done) | copy-start | bytes 6291460
  139.8 2.6 %copy-start.26 = (bf16[2,1024,256]{2,1,0:T(8,128)(2,1)S(1)}, bf16[2,1024,256]{2,1,0:T(8,128)(2,1)}, u32[]{:S(2)}) copy-start(bf16[2,1024,256]{2,1,0:T(8,128)(2,1)} %param.9) | copy-start | bytes 3145732
  142.5 1.2 copy-start.3
  142.5 1.5 %copy-start.4 = (f32[8,128,256]{2,1,0:T(8,128)S(1)}, f32[8,128,256]{2,1,0:T(8,128)}, u32[]{:S(2)}) copy-start(f32[8,128,256]{2,1,0:T(8,128)} %get-tuple-element.5) | copy-start | bytes 3145732
  142.5 1.9 %copy-start.5 = (f32[8,127,256]{2,1,0:T(8,128)S(1)}, f32[8,127,256]{2,1,0:T(8,128)}, u32[]{:S(2)}) copy-start(f32[8,127,256]{2,1,0:T(8,128)} %get-tuple-element.8) | copy-start | bytes 3121156
  142.5 2.2 %copy-start.6 = (f32[8,127,256]{2,1,0:T(8,128)S(1)}, f32[8,127,256]{2,1,0:T(8,128)}, u32[]{:S(2)}) copy-start(f32[8,127,256]{2,1,0:T(8,128)} %get-tuple-element.9) | copy-start | bytes 3121156
  142.5 2.2 %copy-start.16 = (f32[256]{0:T(256)S(1)}, f32[256]{0:T(256)}, u32[]{:S(2)}) copy-start(f32[256]{0:T(256)} %param.11) | copy-start | bytes 3076
  142.5 2.2 %copy-start.18 = (f32[256]{0:T(256)S(1)}, f32[256]{0:T(256)}, u32[]{:S(2)}) copy-start(f32[256]{0:T(256)} %param.10) | copy-start | bytes 3076
  142.5 2.1 %copy-start.19 = (f32[256]{0:T(256)S(1)}, f32[256]{0:T(256)}, u32[]{:S(2)}) copy-start(f32[256]{0:T(256)} %get-tuple-element.22) | copy-start | bytes 3076
  142.5 2.1 %copy-start.20 = (f32[256]{0:T(256)S(1)}, f32[256]{0:T(256)}, u32[]{:S(2)}) copy-start(f32[256]{0:T(256)} %get-tuple-element.24) | copy-start | bytes 3076
Sparse Core Ops, SparseCore 0:
  10.1 48.0 all-gather.3
  60.3 32.0 all-gather.5
  101.5 38.2 all-gather.7
where the time goes:
time: 153 us
  waiting for transfers between devices  79.8 us (52%)
  starting transfers between devices  30.7 us (20%)
  between operations  14 us (9%)
  matrix products  11.3 us (7%)
  other arithmetic  9.25 us (6%)
  local copies, waits for them, and re-layouts  8.15 us (5%)
    all_gather x3, waiting for transfers between devices, products(): piece = lax.all_gather(flat, 'trait', axis=1, tiled=True)  79.7 us
    ppermute x2, starting transfers between devices, with_halo(): lax.ppermute(head, axis, [((i + 1) % count, i) for i in range(count)])  26.7 us
    dot_general x3, matrix products, products(): mutate = jnp.dot(piece, kernels[1], preferred_element_type=jnp.float32)  8.39 us
    convert_element_type x3, other arithmetic, products(): flat = core.astype(jnp.bfloat16).reshape(xcount * ycount, owned)  6.6 us
    ppermute x2, starting transfers between devices, with_halo(): lax.ppermute(tail, axis, [(i, (i + 1) % count) for i in range(count)])  3.84 us
    unnamed x54, local copies, waits for them, and re-layouts  3.7 us
  transfers between devices with their start and end apart: 7, of which 3 were waited for; matrix products, arithmetic and copies ran while one was open for 11% of the time, Pallas kernels for 0%

commit v1 on v0

--- a/solution.py
+++ b/solution.py
@@ -30,7 +30,9 @@
     def products(core):
         xcount, ycount, owned = core.shape
         flat = core.astype(jnp.bfloat16).reshape(xcount * ycount, owned)
-        piece = lax.all_gather(flat, "trait", axis=1, tiled=True)
+        piece = jnp.concatenate(
+            lax.all_to_all(jnp.stack([flat] * lax.axis_size("trait")), "trait", 0, 0), axis=1
+        )
         compete = jnp.dot(piece, kernels[0], preferred_element_type=jnp.float32)
         mutate = jnp.dot(piece, kernels[1], preferred_element_type=jnp.float32)
         compete = compete.astype(jnp.bfloat16)

time: 153 us -> 133 us (0.87)
  waiting for transfers between devices: 79.8 us -> 46.7 us
  starting transfers between devices: 30.7 us -> 47.1 us
  between operations: 14 us -> 1 us
  local copies, waits for them, and re-layouts: 8.15 us -> 14.1 us
  matrix products: 11.3 us -> 16.4 us
  other arithmetic: 9.25 us -> 7.46 us
    all_gather x3 -> x0, waiting for transfers between devices: 79.7 us -> none  [products(): piece = lax.all_gather(flat, 'trait', axis=1, tiled=True)]
    all_to_all x0 -> x3, waiting for transfers between devices: none -> 46.7 us  [products(): lax.all_to_all(jnp.stack([flat] * lax.axis_size('trait')), 'trait', 0, 0)]
    all_to_all x0 -> x3, starting transfers between devices: none -> 22.1 us  [products(): lax.all_to_all(jnp.stack([flat] * lax.axis_size('trait')), 'trait', 0, 0)]
    another operation x0 -> x4, local copies, waits for them, and re-layouts: none -> 8.32 us  [products(): jnp.stack([flat] * lax.axis_size('trait'))]
    ppermute x2, starting transfers between devices: 26.7 us -> 21.1 us  [with_halo(): lax.ppermute(head, axis, [((i + 1) % count, i) for i in range(count)])]
    dot_general x3, matrix products: 2.94 us -> 8.15 us  [products(): compete = jnp.dot(piece, kernels[0], preferred_element_type=jnp.float32)]
    unnamed x54 -> x48, local copies, waits for them, and re-layouts: 3.7 us -> 1.01 us
    convert_element_type x3, other arithmetic: 6.6 us -> 4.86 us  [products(): flat = core.astype(jnp.bfloat16).reshape(xcount * ycount, owned)]
  transfers between devices with their start and end apart: 7 -> 7, of which waited for: 3 -> 3; matrix products, arithmetic and copies ran while one was open for 11% -> 16% of each run, Pallas kernels for 0% -> 0%
where the time goes in v1:
time: 133 us
  starting transfers between devices  47.1 us (35%)
  waiting for transfers between devices  46.7 us (35%)
  matrix products  16.4 us (12%)
  local copies, waits for them, and re-layouts  14.1 us (11%)
  other arithmetic  7.46 us (6%)
    all_to_all x3, waiting for transfers between devices, products(): lax.all_to_all(jnp.stack([flat] * lax.axis_size('trait')), 'trait', 0, 0)  46.7 us
    all_to_all x3, starting transfers between devices, products(): lax.all_to_all(jnp.stack([flat] * lax.axis_size('trait')), 'trait', 0, 0)  22.1 us
    ppermute x2, starting transfers between devices, with_halo(): lax.ppermute(head, axis, [((i + 1) % count, i) for i in range(count)])  21.1 us
    another operation x4, local copies, waits for them, and re-layouts, products(): jnp.stack([flat] * lax.axis_size('trait'))  8.32 us
    dot_general x3, matrix products, products(): mutate = jnp.dot(piece, kernels[1], preferred_element_type=jnp.float32)  8.23 us
    dot_general x3, matrix products, products(): compete = jnp.dot(piece, kernels[0], preferred_element_type=jnp.float32)  8.15 us
    convert_element_type x3, other arithmetic, products(): flat = core.astype(jnp.bfloat16).reshape(xcount * ycount, owned)  4.86 us
    ppermute x2, starting transfers between devices, with_halo(): lax.ppermute(tail, axis, [(i, (i + 1) % count) for i in range(count)])  3.84 us
  transfers between devices with their start and end apart: 7, of which 3 were waited for; matrix products, arithmetic and copies ran while one was open for 16% of the time, Pallas kernels for 0%

profile of v1, /device:TPU:1, one launch (start us, length us, event | category | flops | bytes accessed | tf_op | source)
XLA Modules:
  0.0 132.6 jit_solution(5568908567767292371)
XLA Ops:
  0.6 1.3 convert_element_type.47
  1.9 0.2 copy.9
  2.1 1.6 %stack.22 = bf16[4,1024,256]{1,2,0:T(8,128)(2,1)} broadcast(bf16[1024,256]{0,1:T(8,128)(2,1)S(1)} %copy.9), dimensions={1,2} | broadcast | bytes 2621440 | tf_op jit(solution)/shard_map/stack | solution.py:34
  3.7 11.4 %all-to-all-start.1 = ((bf16[4,1024,256]{1,2,0:T(8,128)(2,1)}), bf16[4,1024,256]{1,2,0:T(8,128)(2,1)}, u32[]{:S(2)}, u32[]{:S(2)}) async-start(bf16[4,1024,256]{1,2,0:T(8,128)(2,1)} %stack.22), calls=%async_computation.1 | async-start | bytes 4194304 | tf_op jit(solution)/shard_map/all_to_all | solution.py:34
  15.1 0.0 copy-done
  15.1 0.1 convert_element_type.43
  15.2 0.2 copy.8
  15.4 24.7 %all-to-all-done.1 = bf16[4,1024,256]{1,2,0:T(8,128)(2,1)} async-done(((bf16[4,1024,256]{1,2,0:T(8,128)(2,1)}), bf16[4,1024,256]{1,2,0:T(8,128)(2,1)}, u32[]{:S(2)}, u32[]{:S(2)}) %all-to-all-start.1) | async-done | bytes 2097184 | tf_op jit(solution)/shard_map/all_to_all | solution.py:34
  40.1 1.6 %stack.21 = bf16[4,1024,256]{1,2,0:T(8,128)(2,1)} broadcast(bf16[1024,256]{0,1:T(8,128)(2,1)S(1)} %copy.8), dimensions={1,2} | broadcast | bytes 2621440 | tf_op jit(solution)/shard_map/stack | solution.py:34
  41.7 5.4 %all-to-all-start = ((bf16[4,1024,256]{1,2,0:T(8,128)(2,1)}), bf16[4,1024,256]{1,2,0:T(8,128)(2,1)}, u32[]{:S(2)}, u32[]{:S(2)}) async-start(bf16[4,1024,256]{1,2,0:T(8,128)(2,1)} %stack.21), calls=%async_computation | async-start | bytes 4194304 | tf_op jit(solution)/shard_map/all_to_all | solution.py:34
  47.1 0.0 copy-done.1
  47.2 10.6 %collective-permute-start = (f32[2,1,128,256]{3,2,1,0:T(8,128)S(1)}, f32[2,1,128,256]{3,2,1,0:T(8,128)S(1)}, u32[]{:S(2)}, u32[]{:S(2)}) collective-permute-start(f32[2,1,128,256]{3,2,1,0:T(8,128)S(1)} %get-tuple-element.6), channel_id=1, source_target_pairs={{4,0},{8,4},{12,8},{16,12},{20,16},{24,20},{28,24},{32,28},{36,32}... | collective-permute-start | bytes 786440 | tf_op jit(solution)/shard_map/ppermute | solution.py:19
  57.8 1.9 %collective-permute-start.1 = (f32[2,1,128,256]{3,2,1,0:T(8,128)S(1)}, f32[2,1,128,256]{3,2,1,0:T(8,128)S(1)}, u32[]{:S(2)}, u32[]{:S(2)}) collective-permute-start(f32[2,1,128,256]{3,2,1,0:T(8,128)S(1)} %get-tuple-element.7), channel_id=1, source_target_pairs={{0,4},{4,8},{8,12},{12,16},{16,20},{20,24},{24,28},{28,32},{32,36}... | collective-permute-start | bytes 786440 | tf_op jit(solution)/shard_map/ppermute | solution.py:17
  59.7 0.0 copy-done.15
  59.7 0.5 broadcast_multiply_fusion
  60.3 0.0 copy-start.21
  60.3 2.1 %fusion.54 = (f32[8,127,256]{2,1,0:T(8,128)}, f32[8,127,256]{2,1,0:T(8,128)}, f32[8,127,256]{2,1,0:T(8,128)}, f32[8,127,256]{2,1,0:T(8,128)}) fusion(f32[8,128,256]{2,1,0:T(8,128)S(1)} %copy-done.1, f32[8,128,256]{2,1,0:T(8,128)S(1)} %copy-done), kind=kLoop, calls=%fused_computation.76 | loop fusion | bytes 8323072 | tf_op jit(solution)/shard_map/jit(_roll_static)/slice | solution.py:47
  62.4 0.0 copy-done.21
  62.4 3.2 %convolution_convert_fusion.2 = bf16[1024,256]{1,0:T(8,128)(2,1)} fusion(bf16[1024,1024]{0,1:T(8,128)(2,1)} %bitcast.14, bf16[2,1024,256]{2,1,0:T(8,128)(2,1)S(1)} %copy-done.21), kind=kOutput, calls=%fused_computation.2 | convolution fusion | flops 537133056 | bytes 3145728 | tf_op jit(solution)/shard_map/dot_general | solution.py:37
  65.6 3.1 %convolution_convert_fusion.3 = bf16[1024,256]{1,0:T(8,128)(2,1)} fusion(bf16[1024,1024]{0,1:T(8,128)(2,1)} %bitcast.14, bf16[2,1024,256]{2,1,0:T(8,128)(2,1)S(1)} %copy-done.21), kind=kOutput, calls=%fused_computation.3 | convolution fusion | flops 537133056 | bytes 3145728 | tf_op jit(solution)/shard_map/dot_general | solution.py:36
  68.8 8.9 %all-to-all-done = bf16[4,1024,256]{1,2,0:T(8,128)(2,1)} async-done(((bf16[4,1024,256]{1,2,0:T(8,128)(2,1)}), bf16[4,1024,256]{1,2,0:T(8,128)(2,1)}, u32[]{:S(2)}, u32[]{:S(2)}) %all-to-all-start) | async-done | bytes 2097184 | tf_op jit(solution)/shard_map/all_to_all | solution.py:34
  77.7 2.5 %convolution_convert_fusion.4 = bf16[1024,256]{1,0:T(8,128)(2,1)S(1)} fusion(bf16[1024,1024]{0,1:T(8,128)(2,1)} %bitcast.5, bf16[2,1024,256]{2,1,0:T(8,128)(2,1)} %param.9), kind=kOutput, calls=%fused_computation.4 | convolution fusion | flops 537133056 | bytes 3145728 | tf_op jit(solution)/shard_map/dot_general | solution.py:37
  80.2 0.0 copy-done.22
  80.2 0.0 copy-start.7
  80.2 0.0 copy-start.8
  80.3 0.0 copy-start.9
  80.3 0.0 copy-start.10
  80.3 0.0 copy-start.11
  80.3 0.0 copy-start.12
  80.3 0.0 copy-start.13
  80.3 0.0 copy-start.17
  80.3 2.5 %convolution_convert_fusion.5 = bf16[1024,256]{1,0:T(8,128)(2,1)S(1)} fusion(bf16[1024,1024]{0,1:T(8,128)(2,1)} %bitcast.5, bf16[2,1024,256]{2,1,0:T(8,128)(2,1)S(1)} %copy-done.22), kind=kOutput, calls=%fused_computation.5 | convolution fusion | flops 537133056 | bytes 3145728 | tf_op jit(solution)/shard_map/dot_general | solution.py:36
  82.8 0.0 collective-permute-done
  82.8 0.0 collective-permute-done.1
  82.8 0.0 copy-start.14
  82.9 0.7 copy-done.14
  83.5 0.0 copy-done.7
  83.6 0.0 copy-done.8
  83.6 0.0 copy-done.9
  83.6 0.0 copy-done.11
  83.6 0.0 copy-done.12
  83.6 0.1 copy-done.13
  83.6 0.0 copy-done.17
  83.6 3.5 %fusion.47 = (bf16[8,128,256]{2,1,0:T(8,128)(2,1)}, f32[8,128,256]{2,1,0:T(8,128)S(1)}, f32[8,128,256]{2,1,0:T(8,128)}, f32[8,128,256]{2,1,0:T(8,128)}) fusion(f32[256]{0:T(256)S(1)} %get-tuple-element.23, f32[8,128,256]{2,1,0:T(8,128)S(1)} %copy-done, f32[256]{0:T(256)S(1)} %copy-done.15, f32[8,128,256]{2,1,0:T(8,128)S(1)} %copy-done.11, ...), kind=kLoop, calls=%fused_computation.71 | loop fusion | flops 13369344 | bytes 15732736 | tf_op jit(solution)/shard_map/convert_element_type | solution.py:32
  87.2 2.4 %copy.10 = bf16[1024,256]{0,1:T(8,128)(2,1)} copy(bf16[1024,256]{1,0:T(8,128)(2,1)} %bitcast.86) | data formatting | bytes 1048576 | tf_op jit(solution)/shard_map/stack;reshape | solution.py:34
  89.6 2.7 %stack.23 = bf16[4,1024,256]{1,2,0:T(8,128)(2,1)} broadcast(bf16[1024,256]{0,1:T(8,128)(2,1)} %copy.10), dimensions={1,2} | broadcast | bytes 2621440 | tf_op jit(solution)/shard_map/stack | solution.py:34
  92.2 5.3 %all-to-all-start.2 = ((bf16[4,1024,256]{1,2,0:T(8,128)(2,1)}), bf16[4,1024,256]{1,2,0:T(8,128)(2,1)}, u32[]{:S(2)}, u32[]{:S(2)}) async-start(bf16[4,1024,256]{1,2,0:T(8,128)(2,1)} %stack.23), calls=%async_computation.2 | async-start | bytes 4194304 | tf_op jit(solution)/shard_map/all_to_all | solution.py:34
  97.5 0.7 fusion.52
  98.2 10.6 %collective-permute-start.2 = (f32[1,128,256]{2,1,0:T(8,128)}, f32[1,128,256]{2,1,0:T(8,128)S(1)}, u32[]{:S(2)}, u32[]{:S(2)}) collective-permute-start(f32[1,128,256]{2,1,0:T(8,128)} %get-tuple-element.12), channel_id=1, source_target_pairs={{4,0},{8,4},{12,8},{16,12},{20,16},{24,20},{28,24},{32,28},{36,32}... | collective-permute-start | bytes 393224 | tf_op jit(solution)/shard_map/ppermute | solution.py:19
  108.7 1.9 %collective-permute-start.3 = (f32[1,128,256]{2,1,0:T(8,128)S(1)}, f32[1,128,256]{2,1,0:T(8,128)S(1)}, u32[]{:S(2)}, u32[]{:S(2)}) collective-permute-start(f32[1,128,256]{2,1,0:T(8,128)S(1)} %get-tuple-element.13), channel_id=1, source_target_pairs={{0,4},{4,8},{8,12},{12,16},{16,20},{20,24},{24,28},{28,32},{32,36}... | collective-permute-start | bytes 393224 | tf_op jit(solution)/shard_map/ppermute | solution.py:17
  110.7 1.5 %fusion.50 = (f32[8,127,256]{2,1,0:T(8,128)}, f32[8,127,256]{2,1,0:T(8,128)}) fusion(f32[8,128,256]{2,1,0:T(8,128)S(1)} %get-tuple-element.3), kind=kLoop, calls=%fused_computation.72 | loop fusion | bytes 4161536 | tf_op jit(solution)/shard_map/jit(_roll_static)/slice | solution.py:47
  112.2 13.1 %all-to-all-done.2 = bf16[4,1024,256]{1,2,0:T(8,128)(2,1)} async-done(((bf16[4,1024,256]{1,2,0:T(8,128)(2,1)}), bf16[4,1024,256]{1,2,0:T(8,128)(2,1)}, u32[]{:S(2)}, u32[]{:S(2)}) %all-to-all-start.2) | async-done | bytes 2097184 | tf_op jit(solution)/shard_map/all_to_all | solution.py:34
  125.3 2.5 %convolution_convert_fusion = bf16[1024,256]{1,0:T(8,128)(2,1)S(1)} fusion(bf16[1024,1024]{0,1:T(8,128)(2,1)} %bitcast.20, bf16[2,1024,256]{2,1,0:T(8,128)(2,1)} %param.9), kind=kOutput, calls=%fused_computation | convolution fusion | flops 537133056 | bytes 3145728 | tf_op jit(solution)/shard_map/dot_general | solution.py:37
  127.8 0.0 copy-done.23
  127.8 0.0 copy-start.3
  127.8 0.0 copy-start.16
  127.8 0.0 copy-start.18
  127.9 2.5 %convolution_convert_fusion.1 = bf16[1024,256]{1,0:T(8,128)(2,1)S(1)} fusion(bf16[1024,1024]{0,1:T(8,128)(2,1)} %bitcast.20, bf16[2,1024,256]{2,1,0:T(8,128)(2,1)S(1)} %copy-done.23), kind=kOutput, calls=%fused_computation.1 | convolution fusion | flops 537133056 | bytes 3145728 | tf_op jit(solution)/shard_map/dot_general | solution.py:36
  130.4 0.0 collective-permute-done.2
  130.4 0.0 collective-permute-done.3
  130.4 0.2 copy-done.6
  130.6 0.0 copy-done.18
  130.6 0.0 copy-done.20
  130.6 2.0 %fusion.13 = f32[8,128,256]{2,1,0:T(8,128)} fusion(f32[8,128,256]{2,1,0:T(8,128)S(1)} %get-tuple-element.3, f32[8,128,256]{2,1,0:T(8,128)S(1)} %copy-done.3, f32[1,128,256]{2,1,0:T(8,128)S(1)} %collective-permute-done.3, f32[1,128,256]{2,1,0:T(8,128)S(1)} %collective-permute-done.2, f32[8,127,256]{2,1,0:T(8,128)S(1)} %copy-done.6, ...), kind=kLoop, calls=%fused_computation.20 | loop fusion | flops 7340032 | bytes 9703424 | tf_op jit(solution)/shard_map/div | solution.py:64
  (21 shorter events, 0.1 us)
Async XLA Ops:
  3.7 11.4 %copy-start = (f32[8,128,256]{2,1,0:T(8,128)S(1)}, f32[8,128,256]{2,1,0:T(8,128)}, u32[]{:S(2)}) copy-start(f32[8,128,256]{2,1,0:T(8,128)} %param.7) | copy-start | bytes 3145732
  3.7 36.3 %all-to-all-start.1 = ((bf16[4,1024,256]{1,2,0:T(8,128)(2,1)}), bf16[4,1024,256]{1,2,0:T(8,128)(2,1)}, u32[]{:S(2)}, u32[]{:S(2)}) async-start(bf16[4,1024,256]{1,2,0:T(8,128)(2,1)} %stack.22), calls=%async_computation.1 | async-start | bytes 4194304 | tf_op jit(solution)/shard_map/all_to_all | solution.py:34
  41.7 5.4 %copy-start.1 = (f32[8,128,256]{2,1,0:T(8,128)S(1)}, f32[8,128,256]{2,1,0:T(8,128)}, u32[]{:S(2)}) copy-start(f32[8,128,256]{2,1,0:T(8,128)} %param.8) | copy-start | bytes 3145732
  41.7 36.0 %all-to-all-start = ((bf16[4,1024,256]{1,2,0:T(8,128)(2,1)}), bf16[4,1024,256]{1,2,0:T(8,128)(2,1)}, u32[]{:S(2)}, u32[]{:S(2)}) async-start(bf16[4,1024,256]{1,2,0:T(8,128)(2,1)} %stack.21), calls=%async_computation | async-start | bytes 4194304 | tf_op jit(solution)/shard_map/all_to_all | solution.py:34
  47.1 12.6 %copy-start.15 = (f32[256]{0:T(256)S(1)}, f32[256]{0:T(256)}, u32[]{:S(2)}) copy-start(f32[256]{0:T(256)} %param.11) | copy-start | bytes 3076
  47.2 35.6 %collective-permute-start = (f32[2,1,128,256]{3,2,1,0:T(8,128)S(1)}, f32[2,1,128,256]{3,2,1,0:T(8,128)S(1)}, u32[]{:S(2)}, u32[]{:S(2)}) collective-permute-start(f32[2,1,128,256]{3,2,1,0:T(8,128)S(1)} %get-tuple-element.6), channel_id=1, source_target_pairs={{4,0},{8,4},{12,8},{16,12},{20,16},{24,20},{28,24},{32,28},{36,32}... | collective-permute-start | bytes 786440 | tf_op jit(solution)/shard_map/ppermute | solution.py:19
  57.8 25.1 %collective-permute-start.1 = (f32[2,1,128,256]{3,2,1,0:T(8,128)S(1)}, f32[2,1,128,256]{3,2,1,0:T(8,128)S(1)}, u32[]{:S(2)}, u32[]{:S(2)}) collective-permute-start(f32[2,1,128,256]{3,2,1,0:T(8,128)S(1)} %get-tuple-element.7), channel_id=1, source_target_pairs={{0,4},{4,8},{8,12},{12,16},{16,20},{20,24},{24,28},{28,32},{32,36}... | collective-permute-start | bytes 786440 | tf_op jit(solution)/shard_map/ppermute | solution.py:17
  60.3 2.2 %copy-start.21 = (bf16[2,1024,256]{2,1,0:T(8,128)(2,1)S(1)}, bf16[2,1024,256]{2,1,0:T(8,128)(2,1)}, u32[]{:S(2)}) copy-start(bf16[2,1024,256]{2,1,0:T(8,128)(2,1)} %param.9) | copy-start | bytes 3145732
  77.7 2.5 %copy-start.22 = (bf16[2,1024,256]{2,1,0:T(8,128)(2,1)S(1)}, bf16[2,1024,256]{2,1,0:T(8,128)(2,1)}, u32[]{:S(2)}) copy-start(bf16[2,1024,256]{2,1,0:T(8,128)(2,1)} %param.9) | copy-start | bytes 3145732
  80.2 3.3 %copy-start.7 = (f32[8,127,256]{2,1,0:T(8,128)S(1)}, f32[8,127,256]{2,1,0:T(8,128)}, u32[]{:S(2)}) copy-start(f32[8,127,256]{2,1,0:T(8,128)} %get-tuple-element.16) | copy-start | bytes 3121156
  80.2 3.3 %copy-start.8 = (f32[8,127,256]{2,1,0:T(8,128)S(1)}, f32[8,127,256]{2,1,0:T(8,128)}, u32[]{:S(2)}) copy-start(f32[8,127,256]{2,1,0:T(8,128)} %get-tuple-element.17) | copy-start | bytes 3121156
  80.3 3.3 %copy-start.9 = (f32[8,127,256]{2,1,0:T(8,128)S(1)}, f32[8,127,256]{2,1,0:T(8,128)}, u32[]{:S(2)}) copy-start(f32[8,127,256]{2,1,0:T(8,128)} %get-tuple-element.28) | copy-start | bytes 3121156
  80.3 3.3 %copy-start.10 = (f32[8,127,256]{2,1,0:T(8,128)S(1)}, f32[8,127,256]{2,1,0:T(8,128)}, u32[]{:S(2)}) copy-start(f32[8,127,256]{2,1,0:T(8,128)} %get-tuple-element.29) | copy-start | bytes 3121156
  80.3 3.3 %copy-start.11 = (f32[8,128,256]{2,1,0:T(8,128)S(1)}, f32[8,128,256]{2,1,0:T(8,128)}, u32[]{:S(2)}) copy-start(f32[8,128,256]{2,1,0:T(8,128)} %param.6) | copy-start | bytes 3145732
  80.3 3.3 %copy-start.12 = (bf16[1024,256]{1,0:T(8,128)(2,1)S(1)}, bf16[1024,256]{1,0:T(8,128)(2,1)}, u32[]{:S(2)}) copy-start(bf16[1024,256]{1,0:T(8,128)(2,1)} %convolution_convert_fusion.2) | copy-start | bytes 1572868
  80.3 3.3 %copy-start.13 = (bf16[1024,256]{1,0:T(8,128)(2,1)S(1)}, bf16[1024,256]{1,0:T(8,128)(2,1)}, u32[]{:S(2)}) copy-start(bf16[1024,256]{1,0:T(8,128)(2,1)} %convolution_convert_fusion.3) | copy-start | bytes 1572868
  80.3 3.3 %copy-start.17 = (f32[256]{0:T(256)S(1)}, f32[256]{0:T(256)}, u32[]{:S(2)}) copy-start(f32[256]{0:T(256)} %param.10) | copy-start | bytes 3076
  82.8 0.7 copy-start.14
  87.2 43.2 %copy-start.2 = (f32[8,128,256]{2,1,0:T(8,128)}, f32[8,128,256]{2,1,0:T(8,128)S(1)}, u32[]{:S(2)}) copy-start(f32[8,128,256]{2,1,0:T(8,128)S(1)} %get-tuple-element.3) | copy-start | bytes 3145732
  92.2 33.0 %all-to-all-start.2 = ((bf16[4,1024,256]{1,2,0:T(8,128)(2,1)}), bf16[4,1024,256]{1,2,0:T(8,128)(2,1)}, u32[]{:S(2)}, u32[]{:S(2)}) async-start(bf16[4,1024,256]{1,2,0:T(8,128)(2,1)} %stack.23), calls=%async_computation.2 | async-start | bytes 4194304 | tf_op jit(solution)/shard_map/all_to_all | solution.py:34
  98.2 32.2 %collective-permute-start.2 = (f32[1,128,256]{2,1,0:T(8,128)}, f32[1,128,256]{2,1,0:T(8,128)S(1)}, u32[]{:S(2)}, u32[]{:S(2)}) collective-permute-start(f32[1,128,256]{2,1,0:T(8,128)} %get-tuple-element.12), channel_id=1, source_target_pairs={{4,0},{8,4},{12,8},{16,12},{20,16},{24,20},{28,24},{32,28},{36,32}... | collective-permute-start | bytes 393224 | tf_op jit(solution)/shard_map/ppermute | solution.py:19
  108.7 21.6 %collective-permute-start.3 = (f32[1,128,256]{2,1,0:T(8,128)S(1)}, f32[1,128,256]{2,1,0:T(8,128)S(1)}, u32[]{:S(2)}, u32[]{:S(2)}) collective-permute-start(f32[1,128,256]{2,1,0:T(8,128)S(1)} %get-tuple-element.13), channel_id=1, source_target_pairs={{0,4},{4,8},{8,12},{12,16},{16,20},{20,24},{24,28},{28,32},{32,36}... | collective-permute-start | bytes 393224 | tf_op jit(solution)/shard_map/ppermute | solution.py:17
  125.3 2.5 %copy-start.23 = (bf16[2,1024,256]{2,1,0:T(8,128)(2,1)S(1)}, bf16[2,1024,256]{2,1,0:T(8,128)(2,1)}, u32[]{:S(2)}) copy-start(bf16[2,1024,256]{2,1,0:T(8,128)(2,1)} %param.9) | copy-start | bytes 3145732
  127.8 2.6 %copy-start.3 = (f32[8,128,256]{2,1,0:T(8,128)S(1)}, f32[8,128,256]{2,1,0:T(8,128)}, u32[]{:S(2)}) copy-start(f32[8,128,256]{2,1,0:T(8,128)} %get-tuple-element.4) | copy-start | bytes 3145732
  127.8 2.6 %copy-start.4 = (f32[8,128,256]{2,1,0:T(8,128)S(1)}, f32[8,128,256]{2,1,0:T(8,128)}, u32[]{:S(2)}) copy-start(f32[8,128,256]{2,1,0:T(8,128)} %get-tuple-element.5) | copy-start | bytes 3145732
  127.8 2.6 %copy-start.5 = (f32[8,127,256]{2,1,0:T(8,128)S(1)}, f32[8,127,256]{2,1,0:T(8,128)}, u32[]{:S(2)}) copy-start(f32[8,127,256]{2,1,0:T(8,128)} %get-tuple-element.8) | copy-start | bytes 3121156
  127.8 2.8 %copy-start.6 = (f32[8,127,256]{2,1,0:T(8,128)S(1)}, f32[8,127,256]{2,1,0:T(8,128)}, u32[]{:S(2)}) copy-start(f32[8,127,256]{2,1,0:T(8,128)} %get-tuple-element.9) | copy-start | bytes 3121156
  127.8 2.8 %copy-start.16 = (f32[256]{0:T(256)S(1)}, f32[256]{0:T(256)}, u32[]{:S(2)}) copy-start(f32[256]{0:T(256)} %param.11) | copy-start | bytes 3076
  127.8 2.8 %copy-start.18 = (f32[256]{0:T(256)S(1)}, f32[256]{0:T(256)}, u32[]{:S(2)}) copy-start(f32[256]{0:T(256)} %param.10) | copy-start | bytes 3076
  127.9 2.8 %copy-start.19 = (f32[256]{0:T(256)S(1)}, f32[256]{0:T(256)}, u32[]{:S(2)}) copy-start(f32[256]{0:T(256)} %get-tuple-element.22) | copy-start | bytes 3076
  127.9 2.7 %copy-start.20 = (f32[256]{0:T(256)S(1)}, f32[256]{0:T(256)}, u32[]{:S(2)}) copy-start(f32[256]{0:T(256)} %get-tuple-element.24) | copy-start | bytes 3076
